TPU v7x, 512 devices: a whole 4x4x16 slice. The times are simulated.
512 devices in a mesh: slab: 16 (over y, x_lo, core), rep: 32 (over z, x_hi).
Axes of the slice: x: 4 (x_hi: 2, x_lo: 2; x = x_hi * 2 + x_lo), y: 4, z: 16, core: 2. Of those that a mesh axis runs over, the one named last changes fastest.
Arguments:
- cells: int32 [16, 65536], P('slab', 'rep'), may hold values from 0 to 262143
- charges: bfloat16 [16, 65536], P('slab', 'rep'), may hold values from 0.5 to 2
- counts: int32 [16, 32], P('slab', 'rep'), may hold values from 1 to 2048, 49152 in all within a row
- potential_guess: float32 [256, 128, 128], P('slab'), may hold values from -6 to 6
Outputs:
- kicks: float32 [3, 16, 65536], P(None, 'slab', 'rep')
Inputs may be any that keep to these rules, and one draw needn't show every extreme that they name: `cells`: a cell is (iz * 128 + ix) * 128 + iy within the macroparticle's own slab. The first counts[s, r] of the 2048 slots of device (s, r) are live; some device holds exactly 2048.
All inputs are finite; a program needn't handle non-finite values.
Results may differ from a plain program's by a relative error of at most 0.003.
Values may be sent and summed in bfloat16 or wider, within the bound.
A program may use at most 64 MiB of HBM per device.

v0:
```python
import jax
import jax.numpy as jnp
from jax import lax
from jax.experimental import pallas as pl
from jax.experimental.pallas import tpu as pltpu
from jax.sharding import PartitionSpec as P

SWEEPS = 8
SCREEN_TERM = 0.05
KICK_STRENGTH = 1.0
DIAG = 6.0 + SCREEN_TERM
PAD = 8
LANES = 128
VMEM_LIMIT = 60 * 1024 * 1024


def coefficients():
    lower = SCREEN_TERM / DIAG
    upper = (12.0 + SCREEN_TERM) / DIAG
    centre = (upper + lower) / 2.0
    radius = (upper - lower) / 2.0
    sigma_ratio = centre / radius
    rho = 1.0 / sigma_ratio
    push = 1.0 / (DIAG * centre)
    result = [(1.0 - push * DIAG, 0.0, push)]
    for _ in range(SWEEPS - 1):
        rho_next = 1.0 / (2.0 * sigma_ratio - rho)
        alpha = rho_next * rho
        push = 2.0 * rho_next / radius / DIAG
        result.append((1.0 + alpha - push * DIAG, alpha, push))
        rho = rho_next
    return result


def deposit_kernel(counts_ref, cells_ref, charges_ref, out_ref):
    total = cells_ref.shape[1]
    rows = out_ref.shape[0]
    cells = cells_ref[...]
    live = lax.broadcasted_iota(jnp.int32, (1, total), 1) < counts_ref[0, 0]
    weights = jnp.where(live, charges_ref[...].astype(jnp.float32), 0.0)
    column = cells & (LANES - 1)
    row = cells >> 7
    spread = jnp.where(
        lax.broadcasted_iota(jnp.int32, (LANES, total), 0) == column, weights, 0.0
    ).astype(jnp.bfloat16)
    block = 256
    iota = lax.broadcasted_iota(jnp.int32, (block, total), 0)
    for start in range(0, rows, block):
        onehot = jnp.where(iota == row - start, 1.0, 0.0).astype(jnp.bfloat16)
        out_ref[start : start + block, :] = lax.dot_general(
            onehot, spread, (((1,), (1,)), ((), ())), preferred_element_type=jnp.float32
        ).astype(out_ref.dtype)


def solve_kernel(
    counts_ref,
    cells_ref,
    guess_ref,
    guess_before_ref,
    guess_after_ref,
    charge_ref,
    charge_before_ref,
    charge_after_ref,
    out_ref,
    even,
    odd,
    charge,
    table,
):
    planes, side, _ = guess_ref.shape
    depth = guess_before_ref.shape[0]
    total = cells_ref.shape[1]
    inside = pl.ds(PAD, side)

    blank = jnp.zeros((PAD, LANES), jnp.float32)

    @pl.loop(0, planes + 2 * depth)
    def _(plane):
        for buffer in (even, odd):
            buffer[plane, pl.ds(0, PAD), :] = blank
            buffer[plane, pl.ds(PAD + side, PAD), :] = blank

    @pl.loop(0, depth)
    def _(plane):
        even[plane, inside, :] = guess_before_ref[plane]
        even[depth + planes + plane, inside, :] = guess_after_ref[plane]

    @pl.loop(0, planes)
    def _(plane):
        even[depth + plane, inside, :] = guess_ref[plane]
        charge[depth - 1 + plane] = charge_ref[plane].astype(jnp.float32)

    @pl.loop(0, depth - 1)
    def _(plane):
        charge[plane] = charge_before_ref[plane].astype(jnp.float32)
        charge[depth - 1 + planes + plane] = charge_after_ref[plane].astype(jnp.float32)

    lane = lax.broadcasted_iota(jnp.int32, (side, LANES), 1)
    first, last = lane == 0, lane == LANES - 1

    def beside(value):
        left = jnp.where(first, 0.0, pltpu.roll(value, 1, 1))
        right = jnp.where(last, 0.0, pltpu.roll(value, LANES - 1, 1))
        return left, right

    buffers = (even, odd)
    for sweep, (keep, previous, push) in enumerate(coefficients()):
        now, later = buffers[sweep % 2], buffers[(sweep + 1) % 2]

        @pl.loop(sweep + 1, planes + 2 * depth - 1 - sweep, unroll=2)
        def _(plane):
            value = now[plane, inside, :]
            left, right = beside(value)
            around = (left + right) + (
                now[plane, pl.ds(PAD - 1, side), :] + now[plane, pl.ds(PAD + 1, side), :]
            )
            around = around + (now[plane - 1, inside, :] + now[plane + 1, inside, :])
            fresh = keep * value + push * (charge[plane - 1] + around)
            if sweep:
                fresh = fresh - previous * later[plane, inside, :]
            later[plane, inside, :] = fresh

    final = buffers[SWEEPS % 2]
    for plane in range(planes):
        at = depth + plane
        spot = slice(plane * LANES, (plane + 1) * LANES)
        left, right = beside(final[at, inside, :])
        parts = (
            final[at, pl.ds(PAD - 1, side), :] - final[at, pl.ds(PAD + 1, side), :],
            left - right,
            final[at - 1, inside, :] - final[at + 1, inside, :],
        )
        for part, difference in enumerate(parts):
            table[part * side : (part + 1) * side, spot] = (difference * 0.5).astype(jnp.bfloat16)

    block = 256
    keys = lax.broadcasted_iota(jnp.int32, (planes * LANES, block), 0)
    ranks = lax.broadcasted_iota(jnp.int32, (side, block), 0)
    for start in range(0, total, block):
        cells = cells_ref[:, start : start + block]
        key = ((cells >> 14) << 7) | (cells & (LANES - 1))
        rank = (cells >> 7) & (LANES - 1)
        onehot = jnp.where(keys == key, 1.0, 0.0).astype(jnp.bfloat16)
        picked = jnp.dot(table[...], onehot, preferred_element_type=jnp.float32)
        slot = lax.broadcasted_iota(jnp.int32, (1, block), 1) + start
        live = slot < counts_ref[0, 0]
        chosen = (ranks == rank) & live
        for part in range(3):
            values = jnp.where(chosen, picked[part * side : (part + 1) * side], 0.0)
            out_ref[part : part + 1, start : start + block] = KICK_STRENGTH * jnp.sum(
                values, axis=0, keepdims=True
            )


def local(cells, charges, counts, potential_guess):
    planes, side, _ = potential_guess.shape
    total = cells.shape[1]
    count = lax.axis_size("slab")
    up = [(i, (i + 1) % count) for i in range(count)]
    down = [(j, i) for i, j in up]
    depth = SWEEPS + 1
    vmem = pl.BlockSpec(memory_space=pltpu.VMEM)
    smem = pl.BlockSpec(memory_space=pltpu.SMEM)
    params = pltpu.CompilerParams(vmem_limit_bytes=VMEM_LIMIT)

    guess_before = lax.ppermute(potential_guess[planes - depth :], "slab", up)
    guess_after = lax.ppermute(potential_guess[:depth], "slab", down)
    deposited = pl.pallas_call(
        deposit_kernel,
        out_shape=jax.ShapeDtypeStruct((planes * side, LANES), jnp.bfloat16),
        in_specs=[smem, vmem, vmem],
        out_specs=vmem,
        compiler_params=params,
        cost_estimate=pl.CostEstimate(flops=2 * planes * side * LANES * total, bytes_accessed=2**19, transcendentals=0),
    )(counts, cells, charges)
    charge = lax.psum(deposited, "rep").reshape(planes, side, LANES)
    charge_before = lax.ppermute(charge[planes - depth + 1 :], "slab", up)
    charge_after = lax.ppermute(charge[: depth - 1], "slab", down)
    deep = planes + 2 * depth
    kicks = pl.pallas_call(
        solve_kernel,
        out_shape=jax.ShapeDtypeStruct((3, total), jnp.float32),
        in_specs=[smem] + [vmem] * 7,
        out_specs=vmem,
        scratch_shapes=[
            pltpu.VMEM((deep, side + 2 * PAD, LANES), jnp.float32),
            pltpu.VMEM((deep, side + 2 * PAD, LANES), jnp.float32),
            pltpu.VMEM((deep - 2, side, LANES), jnp.float32),
            pltpu.VMEM((3 * side, planes * LANES), jnp.bfloat16),
        ],
        compiler_params=params,
    )(counts, cells, potential_guess, guess_before, guess_after, charge, charge_before, charge_after)
    return kicks.reshape(3, 1, total)


def solution(mesh):
    return jax.shard_map(
        local,
        mesh=mesh,
        in_specs=(P("slab", "rep"), P("slab", "rep"), P("slab", "rep"), P("slab", None, None)),
        out_specs=P(None, "slab", "rep"),
        check_vma=False,
    )
```

profile of v0, /device:TPU:1, one launch (start us, length us, event | category | flops | bytes accessed | tf_op | source)
XLA Modules:
  0.0 370.5 jit_solution(2317309580297967678)
XLA Ops:
  6.5 0.0 all-reduce.2.cloned.1.call-start
  7.2 0.0 copy-start
  7.2 3.9 %shard_map.46 = bf16[2048,128]{1,0:T(8,128)(2,1)} custom-call(s32[1,1]{1,0:T(1,128)S(6)} %copy.7.counts_ref, s32[1,2048]{1,0:T(1,128)} %cells_ref.3, bf16[1,2048]{1,0:T(2,128)(2,1)} %charges_ref.1), custom_call_target="tpu_custom_call" | custom-call | flops 1073741824 | bytes 524288 | tf_op jit(solution)/shard_map/pallas_call | solution.py:168
  11.1 0.0 all-reduce.2.cloned.1.call-update
  11.1 0.0 copy-done
  11.2 0.1 fusion
  11.3 4.5 %collective-permute-start = (f32[9,128,128]{2,1,0:T(8,128)S(1)}, f32[9,128,128]{2,1,0:T(8,128)S(1)}, u32[]{:S(2)}, u32[]{:S(2)}) collective-permute-start(f32[9,128,128]{2,1,0:T(8,128)S(1)} %get-tuple-element.6), channel_id=1, source_target_pairs={{0,32},{32,64},{64,96},{96,128},{128,160},{160,192},{192,224},{224... | collective-permute-start | bytes 1769480 | tf_op jit(solution)/shard_map/ppermute | solution.py:166
  15.8 6.2 %collective-permute-start.1 = (f32[9,128,128]{2,1,0:T(8,128)S(1)}, f32[9,128,128]{2,1,0:T(8,128)S(1)}, u32[]{:S(2)}, u32[]{:S(2)}) collective-permute-start(f32[9,128,128]{2,1,0:T(8,128)S(1)} %get-tuple-element.5), channel_id=1, source_target_pairs={{32,0},{64,32},{96,64},{128,96},{160,128},{192,160},{224,192},{256... | collective-permute-start | bytes 1769480 | tf_op jit(solution)/shard_map/ppermute | solution.py:167
  22.0 283.5 %all-reduce.2.cloned.1.call-done = bf16[2048,128]{1,0:T(8,128)(2,1)} async-done(((bf16[2048,128]{1,0:T(8,128)(2,1)}), bf16[2048,128]{1,0:T(8,128)(2,1)}) %all-reduce.2.cloned.1.call-update) | async-done | bytes 524304 | tf_op jit(solution)/shard_map/psum | solution.py:176
  305.5 1.1 fusion.1
  306.6 24.5 %collective-permute-start.2 = (bf16[8,128,128]{2,1,0:T(8,128)(2,1)S(1)}, bf16[8,128,128]{2,1,0:T(8,128)(2,1)S(1)}, u32[]{:S(2)}, u32[]{:S(2)}) collective-permute-start(bf16[8,128,128]{2,1,0:T(8,128)(2,1)S(1)} %bitcast.6), channel_id=1, source_target_pairs={{0,32},{32,64},{64,96},{96,128},{128,160},{160,192},{192,224},{224... | collective-permute-start | bytes 786440 | tf_op jit(solution)/shard_map/ppermute | solution.py:177
  331.1 1.9 collective-permute-start.3
  333.0 0.0 collective-permute-done.guess_before_ref
  333.1 0.0 copy-start.1
  333.1 0.0 collective-permute-done.1.guess_after_ref
  333.1 0.0 copy-start.2
  333.1 1.3 collective-permute-done.2.charge_before_ref
  334.4 0.0 copy-start.3
  334.4 5.4 %collective-permute-done.3.charge_after_ref = bf16[8,128,128]{2,1,0:T(8,128)(2,1)S(1)} collective-permute-done((bf16[8,128,128]{2,1,0:T(8,128)(2,1)S(1)}, bf16[8,128,128]{2,1,0:T(8,128)(2,1)S(1)}, u32[]{:S(2)}, u32[]{:S(2)}) %collective-permute-start.3) | collective-permute-done | bytes 262176 | tf_op jit(solution)/shard_map/ppermute | solution.py:178
  339.8 0.0 copy-start.4
  339.8 0.0 copy-done.1
  339.8 0.0 copy-done.2
  339.8 0.0 copy-done.3
  339.8 0.7 copy-done.4
  340.5 21.8 %shard_map.47 = f32[3,2048]{1,0:T(4,128)} custom-call(s32[1,1]{1,0:T(1,128)S(6)} %copy.7.counts_ref, s32[1,2048]{1,0:T(1,128)} %cells_ref.3, f32[16,128,128]{2,1,0:T(8,128)} %guess_ref.1, f32[9,128,128]{2,1,0:T(8,128)} %copy-done.1, f32[9,128,128]{2,1,0:T(8,128)} %copy-done.2, bf16[16,128,128]{2,1,0:T(8,128)(2,1)} %bitcast.4, ...), custom_call_target="tpu_custom_call" | custom-call | tf_op jit(solution)/shard_map/pallas_call | solution.py:180
  362.3 1.4 copy.5
Async XLA Ops:
  6.5 299.0 %all-reduce.2.cloned.1.call-start = ((), (), s32[]{:S(2)}) async-start(), calls=%async_computation | async-start | bytes 1048576 | tf_op jit(solution)/shard_map/psum | solution.py:176
  7.2 4.0 %copy-start = (f32[16,128,128]{2,1,0:T(8,128)S(1)}, f32[16,128,128]{2,1,0:T(8,128)}, u32[]{:S(2)}) copy-start(f32[16,128,128]{2,1,0:T(8,128)} %guess_ref.1) | copy-start | bytes 3145732
  11.3 321.8 %collective-permute-start = (f32[9,128,128]{2,1,0:T(8,128)S(1)}, f32[9,128,128]{2,1,0:T(8,128)S(1)}, u32[]{:S(2)}, u32[]{:S(2)}) collective-permute-start(f32[9,128,128]{2,1,0:T(8,128)S(1)} %get-tuple-element.6), channel_id=1, source_target_pairs={{0,32},{32,64},{64,96},{96,128},{128,160},{160,192},{192,224},{224... | collective-permute-start | bytes 1769480 | tf_op jit(solution)/shard_map/ppermute | solution.py:166
  15.8 317.3 %collective-permute-start.1 = (f32[9,128,128]{2,1,0:T(8,128)S(1)}, f32[9,128,128]{2,1,0:T(8,128)S(1)}, u32[]{:S(2)}, u32[]{:S(2)}) collective-permute-start(f32[9,128,128]{2,1,0:T(8,128)S(1)} %get-tuple-element.5), channel_id=1, source_target_pairs={{32,0},{64,32},{96,64},{128,96},{160,128},{192,160},{224,192},{256... | collective-permute-start | bytes 1769480 | tf_op jit(solution)/shard_map/ppermute | solution.py:167
  306.6 27.8 %collective-permute-start.2 = (bf16[8,128,128]{2,1,0:T(8,128)(2,1)S(1)}, bf16[8,128,128]{2,1,0:T(8,128)(2,1)S(1)}, u32[]{:S(2)}, u32[]{:S(2)}) collective-permute-start(bf16[8,128,128]{2,1,0:T(8,128)(2,1)S(1)} %bitcast.6), channel_id=1, source_target_pairs={{0,32},{32,64},{64,96},{96,128},{128,160},{160,192},{192,224},{224... | collective-permute-start | bytes 786440 | tf_op jit(solution)/shard_map/ppermute | solution.py:177
  331.1 8.7 %collective-permute-start.3 = (bf16[8,128,128]{2,1,0:T(8,128)(2,1)S(1)}, bf16[8,128,128]{2,1,0:T(8,128)(2,1)S(1)}, u32[]{:S(2)}, u32[]{:S(2)}) collective-permute-start(bf16[8,128,128]{2,1,0:T(8,128)(2,1)S(1)} %bitcast.5), channel_id=1, source_target_pairs={{32,0},{64,32},{96,64},{128,96},{160,128},{192,160},{224,192},{256... | collective-permute-start | bytes 786440 | tf_op jit(solution)/shard_map/ppermute | solution.py:178
  333.1 6.7 %copy-start.1 = (f32[9,128,128]{2,1,0:T(8,128)}, f32[9,128,128]{2,1,0:T(8,128)S(1)}, u32[]{:S(2)}) copy-start(f32[9,128,128]{2,1,0:T(8,128)S(1)} %collective-permute-done.guess_before_ref) | copy-start | bytes 1769476
  333.1 6.7 %copy-start.2 = (f32[9,128,128]{2,1,0:T(8,128)}, f32[9,128,128]{2,1,0:T(8,128)S(1)}, u32[]{:S(2)}) copy-start(f32[9,128,128]{2,1,0:T(8,128)S(1)} %collective-permute-done.1.guess_after_ref) | copy-start | bytes 1769476
  334.4 5.4 %copy-start.3 = (bf16[8,128,128]{2,1,0:T(8,128)(2,1)}, bf16[8,128,128]{2,1,0:T(8,128)(2,1)S(1)}, u32[]{:S(2)}) copy-start(bf16[8,128,128]{2,1,0:T(8,128)(2,1)S(1)} %collective-permute-done.2.charge_before_ref) | copy-start | bytes 786436
  339.8 0.7 copy-start.4
Sparse Core Ops, SparseCore 0:
  11.3 294.1 all-reduce.1
where the time goes:
time: 371 us
  waiting for transfers between devices  290 us (78%)
  starting transfers between devices  37.1 us (10%)
  Pallas kernels  25.7 us (7%)
  between operations  14.1 us (4%)
    psum x1, waiting for transfers between devices, local(): charge = lax.psum(deposited, 'rep').reshape(planes, side, LANES)  284 us
    ppermute x1, starting transfers between devices, local(): charge_before = lax.ppermute(charge[planes - depth + 1:], 'slab', up)  24.5 us
    pallas_call x1, Pallas kernels, local(): pl.pallas_call(solve_kernel, out_shape=jax.ShapeDtypeStruct((3, total), j...  21.8 us
  transfers between devices with their start and end apart: 5, of which 3 were waited for; matrix products, arithmetic and copies ran while one was open for 0% of the time, Pallas kernels for 0%

commit v1 on v0

--- a/solution.py
+++ b/solution.py
@@ -50,6 +50,145 @@
         out_ref[start : start + block, :] = lax.dot_general(
             onehot, spread, (((1,), (1,)), ((), ())), preferred_element_type=jnp.float32
         ).astype(out_ref.dtype)
+
+
+CLASS_ROWS = 256
+HALF = CLASS_ROWS // 2
+NEAR = (
+    (2, 0, 0, HALF, 5),
+    (2, 1, 0, HALF, 6),
+    (-2, 0, HALF, HALF, 5),
+    (-2, 1, HALF, HALF, 6),
+    (0, 1, 0, CLASS_ROWS, 0),
+    (1, 1, 0, CLASS_ROWS, 2),
+    (-1, 1, 0, CLASS_ROWS, 4),
+    (1, 0, 0, CLASS_ROWS, 1),
+    (-1, 0, 0, CLASS_ROWS, 3),
+)
+NEAR_SLOTS = 7
+FAR = (2, 1, 3)
+MESH = pl.DeviceIdType.MESH
+
+
+def reduce_kernel(
+    partial_ref,
+    guess_ref,
+    charge_ref,
+    charge_before_ref,
+    charge_after_ref,
+    guess_before_ref,
+    guess_after_ref,
+    near_in,
+    far_in,
+    near_sum,
+    near_send,
+    near_recv,
+    far_send,
+    far_recv,
+    spread_send,
+    spread_recv,
+    last_send,
+    last_recv,
+    halo_send,
+    halo_recv,
+):
+    ring = lax.axis_size("rep") // 2
+    rep = lax.axis_index("rep")
+    z, x = rep // 2, lax.rem(rep, 2)
+    slabs = lax.axis_size("slab")
+    slab = lax.axis_index("slab")
+    above, below = lax.rem(slab + 1, slabs), lax.rem(slab + slabs - 1, slabs)
+    planes = guess_ref.shape[0]
+    depth = guess_before_ref.shape[0]
+    half = charge_after_ref.shape[0]
+    piece = CLASS_ROWS // 4
+
+    def place(step, other):
+        return lax.rem(z + step + ring, ring), (1 - x if other else x)
+
+    def rep_of(step, other):
+        to_z, to_x = place(step, other)
+        return to_z * 2 + to_x
+
+    def class_of(step, other):
+        to_z, to_x = place(step, other)
+        return pl.multiple_of((lax.rem(to_z, 4) * 2 + to_x) * CLASS_ROWS, CLASS_ROWS)
+
+    def send(src, dst, send_sem, recv_sem, **target):
+        copy = pltpu.make_async_remote_copy(
+            src_ref=src, dst_ref=dst, send_sem=send_sem, recv_sem=recv_sem,
+            device_id=target, device_id_type=MESH,
+        )
+        copy.start()
+        return copy
+
+    barrier = pltpu.get_barrier_semaphore()
+    for step in FAR:
+        pl.semaphore_signal(barrier, inc=1, device_id={"rep": rep_of(4 * step, 0)}, device_id_type=MESH)
+    for step, other, _, _, _ in NEAR:
+        pl.semaphore_signal(barrier, inc=1, device_id={"rep": rep_of(step, other)}, device_id_type=MESH)
+    for target in (above, below):
+        pl.semaphore_signal(barrier, inc=1, device_id={"slab": target}, device_id_type=MESH)
+    pl.semaphore_wait(barrier, len(FAR) + len(NEAR) + 2)
+
+    near = [
+        send(
+            partial_ref.at[pl.ds(class_of(step, other) + first, rows)],
+            near_in.at[slot, pl.ds(first, rows)],
+            near_send.at[i], near_recv.at[i], rep=rep_of(step, other),
+        )
+        for i, (step, other, first, rows, slot) in enumerate(NEAR)
+    ]
+    halo = [
+        send(guess_ref.at[pl.ds(planes - depth, depth)], guess_before_ref, halo_send.at[0], halo_recv.at[0], slab=above),
+        send(guess_ref.at[pl.ds(0, depth)], guess_after_ref, halo_send.at[1], halo_recv.at[1], slab=below),
+    ]
+    for copy in near:
+        copy.wait_recv()
+    mine = class_of(0, 0)
+    total = partial_ref[pl.ds(mine, CLASS_ROWS), :].astype(jnp.float32)
+    for slot in range(NEAR_SLOTS):
+        total = total + near_in[slot].astype(jnp.float32)
+    near_sum[...] = total.astype(near_sum.dtype)
+
+    lot = z // 4
+    far = []
+    for i, step in enumerate(FAR):
+        start = pl.multiple_of(lax.rem(lot + step, 4) * piece, piece)
+        far.append(
+            send(near_sum.at[pl.ds(start, piece)], far_in.at[i], far_send.at[i], far_recv.at[i], rep=rep_of(4 * step, 0))
+        )
+    for copy in far:
+        copy.wait_recv()
+    own = pl.multiple_of(lot * piece, piece)
+    total = near_sum[pl.ds(own, piece), :].astype(jnp.float32)
+    for i in range(len(FAR)):
+        total = total + far_in[i].astype(jnp.float32)
+    spot = pl.ds(pl.multiple_of(mine + own, piece), piece)
+    charge_ref[spot, :] = total.astype(charge_ref.dtype)
+
+    spreads = [
+        send(charge_ref.at[spot], charge_ref.at[spot], spread_send.at[i], spread_recv.at[i], rep=rep_of(4 * step, 0))
+        for i, step in enumerate(FAR)
+    ]
+    for copy in spreads:
+        copy.wait_recv()
+    lasts = []
+    for i, (step, other, first, rows, _) in enumerate(NEAR):
+        block = charge_ref.at[pl.ds(mine + first, rows)]
+        lasts.append(send(block, block, last_send.at[i], last_recv.at[i], rep=rep_of(step, other)))
+    for copy in lasts:
+        copy.wait_recv()
+    halo.append(
+        send(charge_ref.at[pl.ds(half, half)], charge_before_ref, halo_send.at[2], halo_recv.at[2], slab=above)
+    )
+    halo.append(
+        send(charge_ref.at[pl.ds(0, half)], charge_after_ref, halo_send.at[3], halo_recv.at[3], slab=below)
+    )
+    for copy in halo:
+        copy.wait_recv()
+    for copy in near + far + spreads + lasts + halo:
+        copy.wait_send()
 
 
 def solve_kernel(
@@ -147,7 +286,7 @@
         chosen = (ranks == rank) & live
         for part in range(3):
             values = jnp.where(chosen, picked[part * side : (part + 1) * side], 0.0)
-            out_ref[part : part + 1, start : start + block] = KICK_STRENGTH * jnp.sum(
+            out_ref[part, :, start : start + block] = KICK_STRENGTH * jnp.sum(
                 values, axis=0, keepdims=True
             )
 
@@ -155,16 +294,11 @@
 def local(cells, charges, counts, potential_guess):
     planes, side, _ = potential_guess.shape
     total = cells.shape[1]
-    count = lax.axis_size("slab")
-    up = [(i, (i + 1) % count) for i in range(count)]
-    down = [(j, i) for i, j in up]
     depth = SWEEPS + 1
     vmem = pl.BlockSpec(memory_space=pltpu.VMEM)
     smem = pl.BlockSpec(memory_space=pltpu.SMEM)
     params = pltpu.CompilerParams(vmem_limit_bytes=VMEM_LIMIT)
 
-    guess_before = lax.ppermute(potential_guess[planes - depth :], "slab", up)
-    guess_after = lax.ppermute(potential_guess[:depth], "slab", down)
     deposited = pl.pallas_call(
         deposit_kernel,
         out_shape=jax.ShapeDtypeStruct((planes * side, LANES), jnp.bfloat16),
@@ -173,13 +307,39 @@
         compiler_params=params,
         cost_estimate=pl.CostEstimate(flops=2 * planes * side * LANES * total, bytes_accessed=2**19, transcendentals=0),
     )(counts, cells, charges)
-    charge = lax.psum(deposited, "rep").reshape(planes, side, LANES)
-    charge_before = lax.ppermute(charge[planes - depth + 1 :], "slab", up)
-    charge_after = lax.ppermute(charge[: depth - 1], "slab", down)
+    rows = planes * side
+    half = (depth - 1) * side
+    near = pltpu.SemaphoreType.DMA((len(NEAR),))
+    far = pltpu.SemaphoreType.DMA((len(FAR),))
+    ends = pltpu.SemaphoreType.DMA((4,))
+    charge, charge_before, charge_after, guess_before, guess_after = pl.pallas_call(
+        reduce_kernel,
+        out_shape=[
+            jax.ShapeDtypeStruct((rows, LANES), jnp.bfloat16),
+            jax.ShapeDtypeStruct((half, LANES), jnp.bfloat16),
+            jax.ShapeDtypeStruct((half, LANES), jnp.bfloat16),
+            jax.ShapeDtypeStruct((depth, side, LANES), jnp.float32),
+            jax.ShapeDtypeStruct((depth, side, LANES), jnp.float32),
+        ],
+        in_specs=[vmem] * 2,
+        out_specs=[vmem] * 5,
+        scratch_shapes=[
+            pltpu.VMEM((NEAR_SLOTS, CLASS_ROWS, LANES), jnp.bfloat16),
+            pltpu.VMEM((len(FAR), CLASS_ROWS // 4, LANES), jnp.bfloat16),
+            pltpu.VMEM((CLASS_ROWS, LANES), jnp.bfloat16),
+            near, near, far, far, far, far, near, near, ends, ends,
+        ],
+        compiler_params=pltpu.CompilerParams(
+            vmem_limit_bytes=VMEM_LIMIT, collective_id=0, has_side_effects=True
+        ),
+    )(deposited, potential_guess)
+    charge = charge.reshape(planes, side, LANES)
+    charge_before = charge_before.reshape(depth - 1, side, LANES)
+    charge_after = charge_after.reshape(depth - 1, side, LANES)
     deep = planes + 2 * depth
     kicks = pl.pallas_call(
         solve_kernel,
-        out_shape=jax.ShapeDtypeStruct((3, total), jnp.float32),
+        out_shape=jax.ShapeDtypeStruct((3, 1, total), jnp.float32),
         in_specs=[smem] + [vmem] * 7,
         out_specs=vmem,
         scratch_shapes=[
@@ -190,7 +350,7 @@
         ],
         compiler_params=params,
     )(counts, cells, potential_guess, guess_before, guess_after, charge, charge_before, charge_after)
-    return kicks.reshape(3, 1, total)
+    return kicks
 
 
 def solution(mesh):

time: 371 us -> 80.9 us (0.22)
  waiting for transfers between devices: 290 us -> 0 us
  Pallas kernels: 25.7 us -> 80 us
  starting transfers between devices: 37.1 us -> 0 us
  between operations: 14.1 us -> 0.66 us
    psum x1 -> x0, waiting for transfers between devices: 284 us -> none  [local(): charge = lax.psum(deposited, 'rep').reshape(planes, side, LANES)]
    pallas_call x1 -> x2, Pallas kernels: 21.8 us -> 76.1 us  [the longest x1 54.4 us: local(): pl.pallas_call(reduce_kernel, out_shape=[jax.ShapeDtypeStruct((rows, LANE...]
    ppermute x4 -> x0, starting transfers between devices: 37.1 us -> none  [the longest x1 24.5 us: local(): charge_before = lax.ppermute(charge[planes - depth + 1:], 'slab', up)]
    ppermute x4 -> x0, waiting for transfers between devices: 6.71 us -> none  [the longest x1 5.38 us: local(): charge_after = lax.ppermute(charge[:depth - 1], 'slab', down)]
  transfers between devices with their start and end apart: 5 -> 0, of which waited for: 3 -> 0; matrix products, arithmetic and copies ran while one was open for 0% -> 0% of each run, Pallas kernels for 0% -> 0%
where the time goes in v1:
time: 80.9 us; the launch traced here: 80.7 us
  Pallas kernels  80 us (99%)
    pallas_call x1, Pallas kernels, local(): pl.pallas_call(reduce_kernel, out_shape=[jax.ShapeDtypeStruct((rows, LANE...  54.4 us
    pallas_call x1, Pallas kernels, local(): pl.pallas_call(solve_kernel, out_shape=jax.ShapeDtypeStruct((3, 1, total)...  21.8 us
    pallas_call x1, Pallas kernels, local(): pl.pallas_call(deposit_kernel, out_shape=jax.ShapeDtypeStruct((planes * s...  3.85 us

profile of v1, /device:TPU:1, one launch (start us, length us, event | category | flops | bytes accessed | tf_op | source)
XLA Modules:
  0.0 80.7 jit_solution(7570875508851293241)
XLA Ops:
  0.7 3.9 %shard_map.46.partial_ref = bf16[2048,128]{1,0:T(8,128)(2,1)} custom-call(s32[1,1]{1,0:T(1,128)S(6)} %copy.5.counts_ref, s32[1,2048]{1,0:T(1,128)} %cells_ref.3, bf16[1,2048]{1,0:T(2,128)(2,1)} %charges_ref.1), custom_call_target="tpu_custom_call" | custom-call | flops 1073741824 | bytes 524288 | tf_op jit(solution)/shard_map/pallas_call | solution.py:302
  4.5 54.4 %shard_map.47 = (bf16[2048,128]{1,0:T(8,128)(2,1)}, bf16[1024,128]{1,0:T(8,128)(2,1)}, bf16[1024,128]{1,0:T(8,128)(2,1)}, f32[9,128,128]{2,1,0:T(8,128)}, f32[9,128,128]{2,1,0:T(8,128)}) custom-call(bf16[2048,128]{1,0:T(8,128)(2,1)} %shard_map.46.partial_ref, f32[16,128,128]{2,1,0:T(8,128)} %guess_ref.3), custom_call_target="tpu_custom_call" | custom-call | tf_op jit(solution)/shard_map/pallas_call | solution.py:315
  58.9 21.8 %shard_map.48 = f32[3,1,2048]{2,1,0:T(1,128)} custom-call(s32[1,1]{1,0:T(1,128)S(6)} %copy.5.counts_ref, s32[1,2048]{1,0:T(1,128)} %cells_ref.3, f32[16,128,128]{2,1,0:T(8,128)} %guess_ref.3, f32[9,128,128]{2,1,0:T(8,128)} %get-tuple-element.10.guess_before_ref, f32[9,128,128]{2,1,0:T(8,128)} %get-tuple-element.11.guess_after_ref, ...), custom_call_target="tpu_custom_call" | custom-call | tf_op jit(solution)/shard_map/pallas_call | solution.py:340

commit v2 on v1

--- a/solution.py
+++ b/solution.py
@@ -32,7 +32,7 @@
     return result
 
 
-def deposit_kernel(counts_ref, cells_ref, charges_ref, out_ref):
+def deposit(counts_ref, cells_ref, charges_ref, out_ref):
     total = cells_ref.shape[1]
     rows = out_ref.shape[0]
     cells = cells_ref[...]
@@ -52,35 +52,28 @@
         ).astype(out_ref.dtype)
 
 
-CLASS_ROWS = 256
+CLASS_ROWS = 512
 HALF = CLASS_ROWS // 2
-NEAR = (
-    (2, 0, 0, HALF, 5),
-    (2, 1, 0, HALF, 6),
-    (-2, 0, HALF, HALF, 5),
-    (-2, 1, HALF, HALF, 6),
-    (0, 1, 0, CLASS_ROWS, 0),
-    (1, 1, 0, CLASS_ROWS, 2),
-    (-1, 1, 0, CLASS_ROWS, 4),
-    (1, 0, 0, CLASS_ROWS, 1),
-    (-1, 0, 0, CLASS_ROWS, 3),
-)
-NEAR_SLOTS = 7
-FAR = (2, 1, 3)
+NEAR = ((2, 0, HALF, 2), (-2, HALF, HALF, 2), (1, 0, CLASS_ROWS, 0), (-1, 0, CLASS_ROWS, 1))
+NEAR_SLOTS = 3
+FAR = ((2, 1), (2, 0), (1, 1), (3, 1), (1, 0), (3, 0), (0, 1))
+PIECE = CLASS_ROWS // 8
 MESH = pl.DeviceIdType.MESH
 
 
 def reduce_kernel(
-    partial_ref,
+    counts_ref,
+    cells_ref,
+    charges_ref,
     guess_ref,
     charge_ref,
-    charge_before_ref,
-    charge_after_ref,
+    halo_ref,
     guess_before_ref,
     guess_after_ref,
+    partial_ref,
     near_in,
+    near_sum,
     far_in,
-    near_sum,
     near_send,
     near_recv,
     far_send,
@@ -91,6 +84,8 @@
     last_recv,
     halo_send,
     halo_recv,
+    guess_send,
+    guess_recv,
 ):
     ring = lax.axis_size("rep") // 2
     rep = lax.axis_index("rep")
@@ -100,19 +95,17 @@
     above, below = lax.rem(slab + 1, slabs), lax.rem(slab + slabs - 1, slabs)
     planes = guess_ref.shape[0]
     depth = guess_before_ref.shape[0]
-    half = charge_after_ref.shape[0]
-    piece = CLASS_ROWS // 4
-
-    def place(step, other):
-        return lax.rem(z + step + ring, ring), (1 - x if other else x)
-
-    def rep_of(step, other):
-        to_z, to_x = place(step, other)
-        return to_z * 2 + to_x
-
-    def class_of(step, other):
-        to_z, to_x = place(step, other)
-        return pl.multiple_of((lax.rem(to_z, 4) * 2 + to_x) * CLASS_ROWS, CLASS_ROWS)
+    middle = charge_ref.shape[0] // 2
+
+    def rep_of(step, other=0):
+        return lax.rem(z + step + ring, ring) * 2 + (1 - x if other else x)
+
+    def class_of(step):
+        return pl.multiple_of(lax.rem(z + step + ring, 4) * CLASS_ROWS, CLASS_ROWS)
+
+    def piece_of(step, other):
+        lot = lax.rem(z // 4 + step, 4) * 2 + (1 - x if other else x)
+        return pl.multiple_of(lot * PIECE, PIECE)
 
     def send(src, dst, send_sem, recv_sem, **target):
         copy = pltpu.make_async_remote_copy(
@@ -123,71 +116,79 @@
         return copy
 
     barrier = pltpu.get_barrier_semaphore()
-    for step in FAR:
-        pl.semaphore_signal(barrier, inc=1, device_id={"rep": rep_of(4 * step, 0)}, device_id_type=MESH)
-    for step, other, _, _, _ in NEAR:
-        pl.semaphore_signal(barrier, inc=1, device_id={"rep": rep_of(step, other)}, device_id_type=MESH)
+    for step, other in FAR:
+        pl.semaphore_signal(barrier, inc=1, device_id={"rep": rep_of(4 * step, other)}, device_id_type=MESH)
+    for step, _, _, _ in NEAR:
+        pl.semaphore_signal(barrier, inc=1, device_id={"rep": rep_of(step)}, device_id_type=MESH)
     for target in (above, below):
         pl.semaphore_signal(barrier, inc=1, device_id={"slab": target}, device_id_type=MESH)
+
+    deposit(counts_ref, cells_ref, charges_ref, partial_ref)
     pl.semaphore_wait(barrier, len(FAR) + len(NEAR) + 2)
 
     near = [
         send(
-            partial_ref.at[pl.ds(class_of(step, other) + first, rows)],
+            partial_ref.at[pl.ds(class_of(step) + first, rows)],
             near_in.at[slot, pl.ds(first, rows)],
-            near_send.at[i], near_recv.at[i], rep=rep_of(step, other),
-        )
-        for i, (step, other, first, rows, slot) in enumerate(NEAR)
+            near_send.at[i], near_recv.at[i], rep=rep_of(step),
+        )
+        for i, (step, first, rows, slot) in enumerate(NEAR)
     ]
-    halo = [
-        send(guess_ref.at[pl.ds(planes - depth, depth)], guess_before_ref, halo_send.at[0], halo_recv.at[0], slab=above),
-        send(guess_ref.at[pl.ds(0, depth)], guess_after_ref, halo_send.at[1], halo_recv.at[1], slab=below),
+    guesses = [
+        send(guess_ref.at[pl.ds(planes - depth, depth)], guess_before_ref, guess_send.at[0], guess_recv.at[0], slab=above),
+        send(guess_ref.at[pl.ds(0, depth)], guess_after_ref, guess_send.at[1], guess_recv.at[1], slab=below),
     ]
     for copy in near:
         copy.wait_recv()
-    mine = class_of(0, 0)
+    mine = class_of(0)
     total = partial_ref[pl.ds(mine, CLASS_ROWS), :].astype(jnp.float32)
     for slot in range(NEAR_SLOTS):
         total = total + near_in[slot].astype(jnp.float32)
     near_sum[...] = total.astype(near_sum.dtype)
 
-    lot = z // 4
-    far = []
-    for i, step in enumerate(FAR):
-        start = pl.multiple_of(lax.rem(lot + step, 4) * piece, piece)
-        far.append(
-            send(near_sum.at[pl.ds(start, piece)], far_in.at[i], far_send.at[i], far_recv.at[i], rep=rep_of(4 * step, 0))
-        )
+    far = [
+        send(
+            near_sum.at[pl.ds(piece_of(step, other), PIECE)], far_in.at[i],
+            far_send.at[i], far_recv.at[i], rep=rep_of(4 * step, other),
+        )
+        for i, (step, other) in enumerate(FAR)
+    ]
     for copy in far:
         copy.wait_recv()
-    own = pl.multiple_of(lot * piece, piece)
-    total = near_sum[pl.ds(own, piece), :].astype(jnp.float32)
+    own = piece_of(0, 0)
+    total = near_sum[pl.ds(own, PIECE), :].astype(jnp.float32)
     for i in range(len(FAR)):
         total = total + far_in[i].astype(jnp.float32)
-    spot = pl.ds(pl.multiple_of(mine + own, piece), piece)
+    spot = pl.ds(pl.multiple_of(mine + own, PIECE), PIECE)
     charge_ref[spot, :] = total.astype(charge_ref.dtype)
 
     spreads = [
-        send(charge_ref.at[spot], charge_ref.at[spot], spread_send.at[i], spread_recv.at[i], rep=rep_of(4 * step, 0))
-        for i, step in enumerate(FAR)
+        send(
+            charge_ref.at[spot], charge_ref.at[spot],
+            spread_send.at[i], spread_recv.at[i], rep=rep_of(4 * step, other),
+        )
+        for i, (step, other) in enumerate(FAR)
     ]
     for copy in spreads:
         copy.wait_recv()
     lasts = []
-    for i, (step, other, first, rows, _) in enumerate(NEAR):
+    for i, (step, first, rows, _) in enumerate(NEAR):
         block = charge_ref.at[pl.ds(mine + first, rows)]
-        lasts.append(send(block, block, last_send.at[i], last_recv.at[i], rep=rep_of(step, other)))
-    for copy in lasts:
+        lasts.append(send(block, block, last_send.at[i], last_recv.at[i], rep=rep_of(step)))
+
+    def pass_on(i, start, rows):
+        block = pl.ds(start, rows)
+        target = jnp.where(start < middle, below, above)
+        return send(charge_ref.at[block], halo_ref.at[block], halo_send.at[i], halo_recv.at[i], slab=target)
+
+    halos = [pass_on(len(NEAR), mine, CLASS_ROWS)]
+    for i in (2, 3, 0, 1):
+        step, first, rows, _ = NEAR[i]
+        lasts[i].wait_recv()
+        halos.append(pass_on(i, class_of(-step) + first, rows))
+    for copy in guesses + halos:
         copy.wait_recv()
-    halo.append(
-        send(charge_ref.at[pl.ds(half, half)], charge_before_ref, halo_send.at[2], halo_recv.at[2], slab=above)
-    )
-    halo.append(
-        send(charge_ref.at[pl.ds(0, half)], charge_after_ref, halo_send.at[3], halo_recv.at[3], slab=below)
-    )
-    for copy in halo:
-        copy.wait_recv()
-    for copy in near + far + spreads + lasts + halo:
+    for copy in near + far + spreads + lasts + guesses + halos:
         copy.wait_send()
 
 
@@ -198,8 +199,7 @@
     guess_before_ref,
     guess_after_ref,
     charge_ref,
-    charge_before_ref,
-    charge_after_ref,
+    halo_ref,
     out_ref,
     even,
     odd,
@@ -231,8 +231,8 @@
 
     @pl.loop(0, depth - 1)
     def _(plane):
-        charge[plane] = charge_before_ref[plane].astype(jnp.float32)
-        charge[depth - 1 + planes + plane] = charge_after_ref[plane].astype(jnp.float32)
+        charge[plane] = halo_ref[depth - 1 + plane].astype(jnp.float32)
+        charge[depth - 1 + planes + plane] = halo_ref[plane].astype(jnp.float32)
 
     lane = lax.broadcasted_iota(jnp.int32, (side, LANES), 1)
     first, last = lane == 0, lane == LANES - 1
@@ -299,48 +299,36 @@
     smem = pl.BlockSpec(memory_space=pltpu.SMEM)
     params = pltpu.CompilerParams(vmem_limit_bytes=VMEM_LIMIT)
 
-    deposited = pl.pallas_call(
-        deposit_kernel,
-        out_shape=jax.ShapeDtypeStruct((planes * side, LANES), jnp.bfloat16),
-        in_specs=[smem, vmem, vmem],
-        out_specs=vmem,
-        compiler_params=params,
-        cost_estimate=pl.CostEstimate(flops=2 * planes * side * LANES * total, bytes_accessed=2**19, transcendentals=0),
-    )(counts, cells, charges)
     rows = planes * side
-    half = (depth - 1) * side
     near = pltpu.SemaphoreType.DMA((len(NEAR),))
     far = pltpu.SemaphoreType.DMA((len(FAR),))
-    ends = pltpu.SemaphoreType.DMA((4,))
-    charge, charge_before, charge_after, guess_before, guess_after = pl.pallas_call(
+    halos = pltpu.SemaphoreType.DMA((len(NEAR) + 1,))
+    pair = pltpu.SemaphoreType.DMA((2,))
+    grid = jax.ShapeDtypeStruct((rows, LANES), jnp.bfloat16)
+    ends = jax.ShapeDtypeStruct((depth, side, LANES), jnp.float32)
+    charge, halo, guess_before, guess_after = pl.pallas_call(
         reduce_kernel,
-        out_shape=[
-            jax.ShapeDtypeStruct((rows, LANES), jnp.bfloat16),
-            jax.ShapeDtypeStruct((half, LANES), jnp.bfloat16),
-            jax.ShapeDtypeStruct((half, LANES), jnp.bfloat16),
-            jax.ShapeDtypeStruct((depth, side, LANES), jnp.float32),
-            jax.ShapeDtypeStruct((depth, side, LANES), jnp.float32),
-        ],
-        in_specs=[vmem] * 2,
-        out_specs=[vmem] * 5,
+        out_shape=[grid, grid, ends, ends],
+        in_specs=[smem] + [vmem] * 3,
+        out_specs=[vmem] * 4,
         scratch_shapes=[
+            pltpu.VMEM((rows, LANES), jnp.bfloat16),
             pltpu.VMEM((NEAR_SLOTS, CLASS_ROWS, LANES), jnp.bfloat16),
-            pltpu.VMEM((len(FAR), CLASS_ROWS // 4, LANES), jnp.bfloat16),
             pltpu.VMEM((CLASS_ROWS, LANES), jnp.bfloat16),
-            near, near, far, far, far, far, near, near, ends, ends,
+            pltpu.VMEM((len(FAR), PIECE, LANES), jnp.bfloat16),
+            near, near, far, far, far, far, near, near, halos, halos, pair, pair,
         ],
         compiler_params=pltpu.CompilerParams(
             vmem_limit_bytes=VMEM_LIMIT, collective_id=0, has_side_effects=True
         ),
-    )(deposited, potential_guess)
+    )(counts, cells, charges, potential_guess)
     charge = charge.reshape(planes, side, LANES)
-    charge_before = charge_before.reshape(depth - 1, side, LANES)
-    charge_after = charge_after.reshape(depth - 1, side, LANES)
+    halo = halo.reshape(planes, side, LANES)
     deep = planes + 2 * depth
     kicks = pl.pallas_call(
         solve_kernel,
         out_shape=jax.ShapeDtypeStruct((3, 1, total), jnp.float32),
-        in_specs=[smem] + [vmem] * 7,
+        in_specs=[smem] + [vmem] * 6,
         out_specs=vmem,
         scratch_shapes=[
             pltpu.VMEM((deep, side + 2 * PAD, LANES), jnp.float32),
@@ -349,7 +337,7 @@
             pltpu.VMEM((3 * side, planes * LANES), jnp.bfloat16),
         ],
         compiler_params=params,
-    )(counts, cells, potential_guess, guess_before, guess_after, charge, charge_before, charge_after)
+    )(counts, cells, potential_guess, guess_before, guess_after, charge, halo)
     return kicks
 
 

time: 80.9 us -> 79.8 us (0.986)
  Pallas kernels: 80 us -> 78.3 us
    pallas_call x2 -> x1, Pallas kernels: 58.2 us -> 56.5 us  [local(): pl.pallas_call(reduce_kernel, out_shape=[grid, grid, ends, ends], in_spec...]
where the time goes in v2:
time: 79.8 us; the launch traced here: 79 us
  Pallas kernels  78.3 us (98%)
    pallas_call x1, Pallas kernels, local(): pl.pallas_call(reduce_kernel, out_shape=[grid, grid, ends, ends], in_spec...  56.5 us
    pallas_call x1, Pallas kernels, local(): pl.pallas_call(solve_kernel, out_shape=jax.ShapeDtypeStruct((3, 1, total)...  21.8 us

profile of v2, /device:TPU:1, one launch (start us, length us, event | category | flops | bytes accessed | tf_op | source)
XLA Modules:
  0.0 79.0 jit_solution(13892557981016106347)
XLA Ops:
  0.7 56.5 %shard_map.46 = (bf16[2048,128]{1,0:T(8,128)(2,1)}, bf16[2048,128]{1,0:T(8,128)(2,1)}, f32[9,128,128]{2,1,0:T(8,128)}, f32[9,128,128]{2,1,0:T(8,128)}) custom-call(s32[1,1]{1,0:T(1,128)S(6)} %copy.5.counts_ref, s32[1,2048]{1,0:T(1,128)} %cells_ref.3, bf16[1,2048]{1,0:T(2,128)(2,1)} %charges_ref.1, f32[16,128,128]{2,1,0:T(8,128)} %guess_ref.3), custom_call_target="tpu_custom_call" | custom-call | tf_op jit(solution)/shard_map/pallas_call | solution.py:309
  57.1 21.8 %shard_map.47 = f32[3,1,2048]{2,1,0:T(1,128)} custom-call(s32[1,1]{1,0:T(1,128)S(6)} %copy.5.counts_ref, s32[1,2048]{1,0:T(1,128)} %cells_ref.3, f32[16,128,128]{2,1,0:T(8,128)} %guess_ref.3, f32[9,128,128]{2,1,0:T(8,128)} %get-tuple-element.9.guess_before_ref, f32[9,128,128]{2,1,0:T(8,128)} %get-tuple-element.10.guess_after_ref, ...), custom_call_target="tpu_custom_call" | custom-call | tf_op jit(solution)/shard_map/pallas_call | solution.py:328

commit v3 on v2

--- a/solution.py
+++ b/solution.py
@@ -22,12 +22,12 @@
     sigma_ratio = centre / radius
     rho = 1.0 / sigma_ratio
     push = 1.0 / (DIAG * centre)
-    result = [(1.0 - push * DIAG, 0.0, push)]
+    result = [(0.0, push)]
     for _ in range(SWEEPS - 1):
         rho_next = 1.0 / (2.0 * sigma_ratio - rho)
         alpha = rho_next * rho
         push = 2.0 * rho_next / radius / DIAG
-        result.append((1.0 + alpha - push * DIAG, alpha, push))
+        result.append((alpha, push))
         rho = rho_next
     return result
 
@@ -234,30 +234,32 @@
         charge[plane] = halo_ref[depth - 1 + plane].astype(jnp.float32)
         charge[depth - 1 + planes + plane] = halo_ref[plane].astype(jnp.float32)
 
-    lane = lax.broadcasted_iota(jnp.int32, (side, LANES), 1)
-    first, last = lane == 0, lane == LANES - 1
-
     def beside(value):
+        lane = lax.broadcasted_iota(jnp.int32, value.shape, 1)
+        first, last = lane == 0, lane == LANES - 1
         left = jnp.where(first, 0.0, pltpu.roll(value, 1, 1))
         right = jnp.where(last, 0.0, pltpu.roll(value, LANES - 1, 1))
         return left, right
 
     buffers = (even, odd)
-    for sweep, (keep, previous, push) in enumerate(coefficients()):
+    for sweep, (previous, push) in enumerate(coefficients()):
         now, later = buffers[sweep % 2], buffers[(sweep + 1) % 2]
 
-        @pl.loop(sweep + 1, planes + 2 * depth - 1 - sweep, unroll=2)
-        def _(plane):
-            value = now[plane, inside, :]
-            left, right = beside(value)
-            around = (left + right) + (
-                now[plane, pl.ds(PAD - 1, side), :] + now[plane, pl.ds(PAD + 1, side), :]
-            )
-            around = around + (now[plane - 1, inside, :] + now[plane + 1, inside, :])
-            fresh = keep * value + push * (charge[plane - 1] + around)
-            if sweep:
-                fresh = fresh - previous * later[plane, inside, :]
-            later[plane, inside, :] = fresh
+        for start in range(0, side, 64):
+            rows = pl.ds(PAD + start, 64)
+            lower = now[sweep, rows, :]
+            value = now[sweep + 1, rows, :]
+            for plane in range(sweep + 1, planes + 2 * depth - 1 - sweep):
+                upper = now[plane + 1, rows, :]
+                left, right = beside(value)
+                around = now[plane, pl.ds(PAD + start - 1, 64), :] + now[plane, pl.ds(PAD + start + 1, 64), :]
+                around = around + (lower + upper)
+                around = around + charge[plane - 1, pl.ds(start, 64), :]
+                fresh = push * (around + (left + right))
+                if sweep:
+                    fresh = fresh - previous * later[plane, rows, :]
+                later[plane, rows, :] = fresh
+                lower, value = value, upper
 
     final = buffers[SWEEPS % 2]
     for plane in range(planes):

time: 79.8 us -> 72.1 us (0.904)
  Pallas kernels: 78.3 us -> 70.5 us
    pallas_call x1, Pallas kernels: 21.8 us -> 14 us  [local(): pl.pallas_call(solve_kernel, out_shape=jax.ShapeDtypeStruct((3, 1, total)...]
where the time goes in v3:
time: 72.1 us; the launch traced here: 71.2 us
  Pallas kernels  70.5 us (98%)
    pallas_call x1, Pallas kernels, local(): pl.pallas_call(reduce_kernel, out_shape=[grid, grid, ends, ends], in_spec...  56.5 us
    pallas_call x1, Pallas kernels, local(): pl.pallas_call(solve_kernel, out_shape=jax.ShapeDtypeStruct((3, 1, total)...  14 us

profile of v3, /device:TPU:1, one launch (start us, length us, event | category | flops | bytes accessed | tf_op | source)
XLA Modules:
  0.0 71.2 jit_solution(5417979706302246751)
XLA Ops:
  0.7 56.5 %shard_map.46 = (bf16[2048,128]{1,0:T(8,128)(2,1)}, bf16[2048,128]{1,0:T(8,128)(2,1)}, f32[9,128,128]{2,1,0:T(8,128)}, f32[9,128,128]{2,1,0:T(8,128)}) custom-call(s32[1,1]{1,0:T(1,128)S(6)} %copy.5.counts_ref, s32[1,2048]{1,0:T(1,128)} %cells_ref.3, bf16[1,2048]{1,0:T(2,128)(2,1)} %charges_ref.1, f32[16,128,128]{2,1,0:T(8,128)} %guess_ref.3), custom_call_target="tpu_custom_call" | custom-call | tf_op jit(solution)/shard_map/pallas_call | solution.py:311
  57.1 14.0 %shard_map.47 = f32[3,1,2048]{2,1,0:T(1,128)} custom-call(s32[1,1]{1,0:T(1,128)S(6)} %copy.5.counts_ref, s32[1,2048]{1,0:T(1,128)} %cells_ref.3, f32[16,128,128]{2,1,0:T(8,128)} %guess_ref.3, f32[9,128,128]{2,1,0:T(8,128)} %get-tuple-element.9.guess_before_ref, f32[9,128,128]{2,1,0:T(8,128)} %get-tuple-element.10.guess_after_ref, ...), custom_call_target="tpu_custom_call" | custom-call | tf_op jit(solution)/shard_map/pallas_call | solution.py:330

commit v4 on v3

--- a/solution.py
+++ b/solution.py
@@ -52,12 +52,23 @@
         ).astype(out_ref.dtype)
 
 
-CLASS_ROWS = 512
+CLASS_ROWS = 256
 HALF = CLASS_ROWS // 2
-NEAR = ((2, 0, HALF, 2), (-2, HALF, HALF, 2), (1, 0, CLASS_ROWS, 0), (-1, 0, CLASS_ROWS, 1))
-NEAR_SLOTS = 3
-FAR = ((2, 1), (2, 0), (1, 1), (3, 1), (1, 0), (3, 0), (0, 1))
-PIECE = CLASS_ROWS // 8
+NEAR = (
+    (2, 1, 0, HALF, 6),
+    (-2, 1, HALF, HALF, 6),
+    (1, 1, 0, CLASS_ROWS, 2),
+    (-1, 1, 0, CLASS_ROWS, 4),
+    (0, 1, 0, CLASS_ROWS, 0),
+    (2, 0, 0, HALF, 5),
+    (-2, 0, HALF, HALF, 5),
+    (1, 0, 0, CLASS_ROWS, 1),
+    (-1, 0, 0, CLASS_ROWS, 3),
+)
+NEAR_SLOTS = 7
+ARRIVALS = (7, 8, 4, 5, 6, 2, 3, 0, 1)
+FAR = (2, 1, 3)
+PIECE = CLASS_ROWS // 4
 MESH = pl.DeviceIdType.MESH
 
 
@@ -100,12 +111,12 @@
     def rep_of(step, other=0):
         return lax.rem(z + step + ring, ring) * 2 + (1 - x if other else x)
 
-    def class_of(step):
-        return pl.multiple_of(lax.rem(z + step + ring, 4) * CLASS_ROWS, CLASS_ROWS)
-
-    def piece_of(step, other):
-        lot = lax.rem(z // 4 + step, 4) * 2 + (1 - x if other else x)
-        return pl.multiple_of(lot * PIECE, PIECE)
+    def class_of(step, other=0):
+        lot = lax.rem(z + step + ring, 4) * 2 + (1 - x if other else x)
+        return pl.multiple_of(lot * CLASS_ROWS, CLASS_ROWS)
+
+    def piece_of(step):
+        return pl.multiple_of(lax.rem(z // 4 + step, 4) * PIECE, PIECE)
 
     def send(src, dst, send_sem, recv_sem, **target):
         copy = pltpu.make_async_remote_copy(
@@ -116,10 +127,10 @@
         return copy
 
     barrier = pltpu.get_barrier_semaphore()
-    for step, other in FAR:
-        pl.semaphore_signal(barrier, inc=1, device_id={"rep": rep_of(4 * step, other)}, device_id_type=MESH)
-    for step, _, _, _ in NEAR:
-        pl.semaphore_signal(barrier, inc=1, device_id={"rep": rep_of(step)}, device_id_type=MESH)
+    for step in FAR:
+        pl.semaphore_signal(barrier, inc=1, device_id={"rep": rep_of(4 * step)}, device_id_type=MESH)
+    for step, other, _, _, _ in NEAR:
+        pl.semaphore_signal(barrier, inc=1, device_id={"rep": rep_of(step, other)}, device_id_type=MESH)
     for target in (above, below):
         pl.semaphore_signal(barrier, inc=1, device_id={"slab": target}, device_id_type=MESH)
 
@@ -128,15 +139,11 @@
 
     near = [
         send(
-            partial_ref.at[pl.ds(class_of(step) + first, rows)],
+            partial_ref.at[pl.ds(class_of(step, other) + first, rows)],
             near_in.at[slot, pl.ds(first, rows)],
-            near_send.at[i], near_recv.at[i], rep=rep_of(step),
-        )
-        for i, (step, first, rows, slot) in enumerate(NEAR)
-    ]
-    guesses = [
-        send(guess_ref.at[pl.ds(planes - depth, depth)], guess_before_ref, guess_send.at[0], guess_recv.at[0], slab=above),
-        send(guess_ref.at[pl.ds(0, depth)], guess_after_ref, guess_send.at[1], guess_recv.at[1], slab=below),
+            near_send.at[i], near_recv.at[i], rep=rep_of(step, other),
+        )
+        for i, (step, other, first, rows, slot) in enumerate(NEAR)
     ]
     for copy in near:
         copy.wait_recv()
@@ -148,14 +155,18 @@
 
     far = [
         send(
-            near_sum.at[pl.ds(piece_of(step, other), PIECE)], far_in.at[i],
-            far_send.at[i], far_recv.at[i], rep=rep_of(4 * step, other),
-        )
-        for i, (step, other) in enumerate(FAR)
+            near_sum.at[pl.ds(piece_of(step), PIECE)], far_in.at[i],
+            far_send.at[i], far_recv.at[i], rep=rep_of(4 * step),
+        )
+        for i, step in enumerate(FAR)
+    ]
+    guesses = [
+        send(guess_ref.at[pl.ds(planes - depth, depth)], guess_before_ref, guess_send.at[0], guess_recv.at[0], slab=above),
+        send(guess_ref.at[pl.ds(0, depth)], guess_after_ref, guess_send.at[1], guess_recv.at[1], slab=below),
     ]
     for copy in far:
         copy.wait_recv()
-    own = piece_of(0, 0)
+    own = piece_of(0)
     total = near_sum[pl.ds(own, PIECE), :].astype(jnp.float32)
     for i in range(len(FAR)):
         total = total + far_in[i].astype(jnp.float32)
@@ -165,16 +176,16 @@
     spreads = [
         send(
             charge_ref.at[spot], charge_ref.at[spot],
-            spread_send.at[i], spread_recv.at[i], rep=rep_of(4 * step, other),
-        )
-        for i, (step, other) in enumerate(FAR)
+            spread_send.at[i], spread_recv.at[i], rep=rep_of(4 * step),
+        )
+        for i, step in enumerate(FAR)
     ]
     for copy in spreads:
         copy.wait_recv()
     lasts = []
-    for i, (step, first, rows, _) in enumerate(NEAR):
+    for i, (step, other, first, rows, _) in enumerate(NEAR):
         block = charge_ref.at[pl.ds(mine + first, rows)]
-        lasts.append(send(block, block, last_send.at[i], last_recv.at[i], rep=rep_of(step)))
+        lasts.append(send(block, block, last_send.at[i], last_recv.at[i], rep=rep_of(step, other)))
 
     def pass_on(i, start, rows):
         block = pl.ds(start, rows)
@@ -182,10 +193,10 @@
         return send(charge_ref.at[block], halo_ref.at[block], halo_send.at[i], halo_recv.at[i], slab=target)
 
     halos = [pass_on(len(NEAR), mine, CLASS_ROWS)]
-    for i in (2, 3, 0, 1):
-        step, first, rows, _ = NEAR[i]
+    for i in ARRIVALS:
+        step, other, first, rows, _ = NEAR[i]
         lasts[i].wait_recv()
-        halos.append(pass_on(i, class_of(-step) + first, rows))
+        halos.append(pass_on(i, class_of(-step, other) + first, rows))
     for copy in guesses + halos:
         copy.wait_recv()
     for copy in near + far + spreads + lasts + guesses + halos:
@@ -275,13 +286,13 @@
             table[part * side : (part + 1) * side, spot] = (difference * 0.5).astype(jnp.bfloat16)
 
     block = 256
-    keys = lax.broadcasted_iota(jnp.int32, (planes * LANES, block), 0)
+    keys = lax.broadcasted_iota(jnp.int16, (planes * LANES, block), 0)
     ranks = lax.broadcasted_iota(jnp.int32, (side, block), 0)
     for start in range(0, total, block):
         cells = cells_ref[:, start : start + block]
         key = ((cells >> 14) << 7) | (cells & (LANES - 1))
         rank = (cells >> 7) & (LANES - 1)
-        onehot = jnp.where(keys == key, 1.0, 0.0).astype(jnp.bfloat16)
+        onehot = jnp.where(keys == key.astype(jnp.int16), jnp.bfloat16(1.0), jnp.bfloat16(0.0))
         picked = jnp.dot(table[...], onehot, preferred_element_type=jnp.float32)
         slot = lax.broadcasted_iota(jnp.int32, (1, block), 1) + start
         live = slot < counts_ref[0, 0]

time: 72.1 us -> 67.5 us (0.936); the launches traced: 71.2 us -> 67.3 us
  Pallas kernels: 70.5 us -> 66.7 us
    pallas_call x1, Pallas kernels: 56.5 us -> 53 us  [local(): pl.pallas_call(reduce_kernel, out_shape=[grid, grid, ends, ends], in_spec...]
where the time goes in v4:
time: 67.5 us; the launch traced here: 67.3 us
  Pallas kernels  66.7 us (99%)
    pallas_call x1, Pallas kernels, local(): pl.pallas_call(reduce_kernel, out_shape=[grid, grid, ends, ends], in_spec...  53 us
    pallas_call x1, Pallas kernels, local(): pl.pallas_call(solve_kernel, out_shape=jax.ShapeDtypeStruct((3, 1, total)...  13.7 us

profile of v4, /device:TPU:1, one launch (start us, length us, event | category | flops | bytes accessed | tf_op | source)
XLA Modules:
  0.0 67.3 jit_solution(13975388690055126232)
XLA Ops:
  0.7 53.0 %shard_map.46 = (bf16[2048,128]{1,0:T(8,128)(2,1)}, bf16[2048,128]{1,0:T(8,128)(2,1)}, f32[9,128,128]{2,1,0:T(8,128)}, f32[9,128,128]{2,1,0:T(8,128)}) custom-call(s32[1,1]{1,0:T(1,128)S(6)} %copy.5.counts_ref, s32[1,2048]{1,0:T(1,128)} %cells_ref.3, bf16[1,2048]{1,0:T(2,128)(2,1)} %charges_ref.1, f32[16,128,128]{2,1,0:T(8,128)} %guess_ref.3), custom_call_target="tpu_custom_call" | custom-call | tf_op jit(solution)/shard_map/pallas_call | solution.py:322
  53.6 13.7 %shard_map.47 = f32[3,1,2048]{2,1,0:T(1,128)} custom-call(s32[1,1]{1,0:T(1,128)S(6)} %copy.5.counts_ref, s32[1,2048]{1,0:T(1,128)} %cells_ref.3, f32[16,128,128]{2,1,0:T(8,128)} %guess_ref.3, f32[9,128,128]{2,1,0:T(8,128)} %get-tuple-element.9.guess_before_ref, f32[9,128,128]{2,1,0:T(8,128)} %get-tuple-element.10.guess_after_ref, ...), custom_call_target="tpu_custom_call" | custom-call | tf_op jit(solution)/shard_map/pallas_call | solution.py:341

commit v5 on v4

--- a/solution.py
+++ b/solution.py
@@ -66,7 +66,7 @@
     (-1, 0, 0, CLASS_ROWS, 3),
 )
 NEAR_SLOTS = 7
-ARRIVALS = (7, 8, 4, 5, 6, 2, 3, 0, 1)
+SHARE = ((1, 0), (-1, 0), (0, 1), (2, 0), (1, 1), (-1, 1), (2, 1))
 FAR = (2, 1, 3)
 PIECE = CLASS_ROWS // 4
 MESH = pl.DeviceIdType.MESH
@@ -180,23 +180,33 @@
         )
         for i, step in enumerate(FAR)
     ]
-    for copy in spreads:
-        copy.wait_recv()
-    lasts = []
-    for i, (step, other, first, rows, _) in enumerate(NEAR):
-        block = charge_ref.at[pl.ds(mine + first, rows)]
-        lasts.append(send(block, block, last_send.at[i], last_recv.at[i], rep=rep_of(step, other)))
-
-    def pass_on(i, start, rows):
-        block = pl.ds(start, rows)
+    def share(piece, order):
+        block = charge_ref.at[pl.ds(pl.multiple_of(mine + piece * PIECE, PIECE), PIECE)]
+        for i in reversed(range(len(SHARE))):
+            step, other = SHARE[i]
+            if step == 2:
+                step = jnp.where(piece < 2, 2, -2)
+            lasts[i].append(
+                send(block, block, last_send.at[i, order], last_recv.at[i, piece], rep=rep_of(step, other))
+            )
+
+    def pass_on(i, start):
+        block = pl.ds(start, CLASS_ROWS)
         target = jnp.where(start < middle, below, above)
         return send(charge_ref.at[block], halo_ref.at[block], halo_send.at[i], halo_recv.at[i], slab=target)
 
-    halos = [pass_on(len(NEAR), mine, CLASS_ROWS)]
-    for i in ARRIVALS:
-        step, other, first, rows, _ = NEAR[i]
-        lasts[i].wait_recv()
-        halos.append(pass_on(i, class_of(-step, other) + first, rows))
+    lasts = [[] for _ in SHARE]
+    lot = z // 4
+    share(lot, 0)
+    for order, i in enumerate((1, 2, 0)):
+        spreads[i].wait_recv()
+        share(lax.rem(lot + 4 - FAR[i], 4), order + 1)
+    halos = [pass_on(len(SHARE), mine)]
+    for i, (step, other) in enumerate(SHARE):
+        for copy in lasts[i]:
+            copy.wait_recv()
+        halos.append(pass_on(i, class_of(-step, other)))
+    lasts = [copy for copies in lasts for copy in copies]
     for copy in guesses + halos:
         copy.wait_recv()
     for copy in near + far + spreads + lasts + guesses + halos:
@@ -315,7 +325,8 @@
     rows = planes * side
     near = pltpu.SemaphoreType.DMA((len(NEAR),))
     far = pltpu.SemaphoreType.DMA((len(FAR),))
-    halos = pltpu.SemaphoreType.DMA((len(NEAR) + 1,))
+    share = pltpu.SemaphoreType.DMA((len(SHARE), 4))
+    halos = pltpu.SemaphoreType.DMA((len(SHARE) + 1,))
     pair = pltpu.SemaphoreType.DMA((2,))
     grid = jax.ShapeDtypeStruct((rows, LANES), jnp.bfloat16)
     ends = jax.ShapeDtypeStruct((depth, side, LANES), jnp.float32)
@@ -329,7 +340,7 @@
             pltpu.VMEM((NEAR_SLOTS, CLASS_ROWS, LANES), jnp.bfloat16),
             pltpu.VMEM((CLASS_ROWS, LANES), jnp.bfloat16),
             pltpu.VMEM((len(FAR), PIECE, LANES), jnp.bfloat16),
-            near, near, far, far, far, far, near, near, halos, halos, pair, pair,
+            near, near, far, far, far, far, share, share, halos, halos, pair, pair,
         ],
         compiler_params=pltpu.CompilerParams(
             vmem_limit_bytes=VMEM_LIMIT, collective_id=0, has_side_effects=True

time: 67.5 us -> 68.1 us (level)
  no operation moved by 1% of the time
where the time goes in v5:
time: 68.1 us; the launch traced here: 67.6 us
  Pallas kernels  67 us (98%)
    pallas_call x1, Pallas kernels, local(): pl.pallas_call(reduce_kernel, out_shape=[grid, grid, ends, ends], in_spec...  53.3 us
    pallas_call x1, Pallas kernels, local(): pl.pallas_call(solve_kernel, out_shape=jax.ShapeDtypeStruct((3, 1, total)...  13.7 us

profile of v5, /device:TPU:1, one launch (start us, length us, event | category | flops | bytes accessed | tf_op | source)
XLA Modules:
  0.0 67.6 jit_solution(12334653578851428347)
XLA Ops:
  0.7 53.3 %shard_map.46 = (bf16[2048,128]{1,0:T(8,128)(2,1)}, bf16[2048,128]{1,0:T(8,128)(2,1)}, f32[9,128,128]{2,1,0:T(8,128)}, f32[9,128,128]{2,1,0:T(8,128)}) custom-call(s32[1,1]{1,0:T(1,128)S(6)} %copy.5.counts_ref, s32[1,2048]{1,0:T(1,128)} %cells_ref.3, bf16[1,2048]{1,0:T(2,128)(2,1)} %charges_ref.1, f32[16,128,128]{2,1,0:T(8,128)} %guess_ref.3), custom_call_target="tpu_custom_call" | custom-call | tf_op jit(solution)/shard_map/pallas_call | solution.py:333
  54.0 13.7 %shard_map.47 = f32[3,1,2048]{2,1,0:T(1,128)} custom-call(s32[1,1]{1,0:T(1,128)S(6)} %copy.5.counts_ref, s32[1,2048]{1,0:T(1,128)} %cells_ref.3, f32[16,128,128]{2,1,0:T(8,128)} %guess_ref.3, f32[9,128,128]{2,1,0:T(8,128)} %get-tuple-element.9.guess_before_ref, f32[9,128,128]{2,1,0:T(8,128)} %get-tuple-element.10.guess_after_ref, ...), custom_call_target="tpu_custom_call" | custom-call | tf_op jit(solution)/shard_map/pallas_call | solution.py:352

commit v6 on v4

--- a/solution.py
+++ b/solution.py
@@ -310,6 +310,7 @@
     depth = SWEEPS + 1
     vmem = pl.BlockSpec(memory_space=pltpu.VMEM)
     smem = pl.BlockSpec(memory_space=pltpu.SMEM)
+    outside = pl.BlockSpec(memory_space=pl.ANY)
     params = pltpu.CompilerParams(vmem_limit_bytes=VMEM_LIMIT)
 
     rows = planes * side
@@ -322,8 +323,8 @@
     charge, halo, guess_before, guess_after = pl.pallas_call(
         reduce_kernel,
         out_shape=[grid, grid, ends, ends],
-        in_specs=[smem] + [vmem] * 3,
-        out_specs=[vmem] * 4,
+        in_specs=[smem, vmem, vmem, outside],
+        out_specs=[vmem, vmem, outside, outside],
         scratch_shapes=[
             pltpu.VMEM((rows, LANES), jnp.bfloat16),
             pltpu.VMEM((NEAR_SLOTS, CLASS_ROWS, LANES), jnp.bfloat16),

time: 67.5 us -> 66.8 us (0.990)
  Pallas kernels: 66.7 us -> 66 us
    pallas_call x1, Pallas kernels: 53 us -> 52.3 us  [local(): pl.pallas_call(reduce_kernel, out_shape=[grid, grid, ends, ends], in_spec...]
where the time goes in v6:
time: 66.8 us; the launch traced here: 66.6 us
  Pallas kernels  66 us (99%)
    pallas_call x1, Pallas kernels, local(): pl.pallas_call(reduce_kernel, out_shape=[grid, grid, ends, ends], in_spec...  52.3 us
    pallas_call x1, Pallas kernels, local(): pl.pallas_call(solve_kernel, out_shape=jax.ShapeDtypeStruct((3, 1, total)...  13.7 us

profile of v6, /device:TPU:1, one launch (start us, length us, event | category | flops | bytes accessed | tf_op | source)
XLA Modules:
  0.0 66.6 jit_solution(7509199603354253382)
XLA Ops:
  0.7 52.3 %shard_map.46 = (bf16[2048,128]{1,0:T(8,128)(2,1)}, bf16[2048,128]{1,0:T(8,128)(2,1)}, f32[9,128,128]{2,1,0:T(8,128)}, f32[9,128,128]{2,1,0:T(8,128)}) custom-call(s32[1,1]{1,0:T(1,128)S(6)} %copy.5.counts_ref, s32[1,2048]{1,0:T(1,128)} %cells_ref.3, bf16[1,2048]{1,0:T(2,128)(2,1)} %charges_ref.1, f32[16,128,128]{2,1,0:T(8,128)} %guess_ref.3), custom_call_target="tpu_custom_call" | custom-call | tf_op jit(solution)/shard_map/pallas_call | solution.py:323
  52.9 13.7 %shard_map.47 = f32[3,1,2048]{2,1,0:T(1,128)} custom-call(s32[1,1]{1,0:T(1,128)S(6)} %copy.5.counts_ref, s32[1,2048]{1,0:T(1,128)} %cells_ref.3, f32[16,128,128]{2,1,0:T(8,128)} %guess_ref.3, f32[9,128,128]{2,1,0:T(8,128)} %get-tuple-element.9.guess_before_ref, f32[9,128,128]{2,1,0:T(8,128)} %get-tuple-element.10.guess_after_ref, ...), custom_call_target="tpu_custom_call" | custom-call | tf_op jit(solution)/shard_map/pallas_call | solution.py:342
